TPU v7x, 128 devices: a whole 4x4x4 slice. The times are simulated.
128 devices in a mesh: dp: 32 (over z_lo, x, y), tensor: 4 (over z_hi, core).
Axes of the slice: x: 4, y: 4, z: 4 (z_hi: 2, z_lo: 2; z = z_hi * 2 + z_lo), core: 2. Of those that a mesh axis runs over, the one named last changes fastest.
Arguments:
- hidden: bfloat16 [64, 512, 5120], P('dp'), may hold values from -5 to 5
- query_projection_matrix: bfloat16 [5120, 2560], P('dp', 'tensor'), may hold values from -0.5 to 0.5
- key_projection_matrix: bfloat16 [5120, 2560], P('dp', 'tensor'), may hold values from -0.5 to 0.5
- value_projection_matrix: bfloat16 [5120, 2560], P('dp', 'tensor'), may hold values from -0.078125 to 0.078125
- adapter_down_maps: bfloat16 [2, 8, 5120], replicated, may hold values from -0.078125 to 0.078125
- adapter_up_maps: bfloat16 [2, 8, 2560], P(None, None, 'tensor'), may hold values from -1 to 1
- cotangent: bfloat16 [64, 512, 2560], P('dp', None, 'tensor'), may hold values from -6 to 6
- lengths: int32 [64], P('dp'), may hold values from 1 to 512, 16640 in all
- random_signs_down: bfloat16 [2, 8, 5120, 4096], P(None, None, ('dp', 'tensor')), may hold values from -4 to 4
- random_signs_up: bfloat16 [2, 8, 20, 128, 4096], P(None, None, 'tensor', 'dp'), may hold values from -4 to 4
Outputs:
- features: float32 [64, 4096], P('dp', 'tensor')
Inputs may be any that keep to these rules, and one draw needn't show every extreme that they name: `lengths`: positions at or beyond an example's length are padding.
All inputs are finite; a program needn't handle non-finite values. No bound on the sum of `lengths` on one device may be relied on, other than what follows from the above.
Results may differ from a plain program's by a relative error of at most 0.025.
Values may be sent and summed in bfloat16 or wider, within the bound.
A program may use at most 128 MiB of HBM per device.

v0:
```python
import jax
import jax.numpy as jnp
from jax import lax
from jax.sharding import Mesh, PartitionSpec as P

HEAD_DIM = 128
ADAPTER_RANK = 8
FEAT = 4096
DP_AXES = ("zl", "x", "y")
TP_AXES = ("zh", "core")
adapter_scale = 2.0
rope_base = 10000.0
norm_eps = 1e-05
masked_score = -1e30


def rope_tables(seq_len, head_width):
    half_width = head_width // 2
    frequency = rope_base ** (-2.0 * jnp.arange(half_width, dtype=jnp.float32) / head_width)
    angles = jnp.arange(seq_len, dtype=jnp.float32)[:, None] * frequency[None, :]
    rotary_cosines = jnp.concatenate([jnp.cos(angles), jnp.cos(angles)], axis=1)
    rotary_sines = jnp.concatenate([jnp.sin(angles), jnp.sin(angles)], axis=1)
    return (rotary_cosines, rotary_sines)


def apply_rotary(tensor_in, rotary_cosines, rotary_sines):
    half_width = tensor_in.shape[-1] // 2
    turned = jnp.concatenate([-tensor_in[..., half_width:], tensor_in[..., :half_width]], axis=-1)
    return tensor_in * rotary_cosines[:, None, :] + turned * rotary_sines[:, None, :]


def unrotate(gradient, rotary_cosines, rotary_sines):
    half_width = gradient.shape[-1] // 2
    scaled = gradient * rotary_sines[:, None, :]
    rotated_back = jnp.concatenate([scaled[..., half_width:], -scaled[..., :half_width]], axis=-1)
    return gradient * rotary_cosines[:, None, :] + rotated_back


def attention_grads(example):
    query_per_head, key_heads, value_per_head, grad_out, seq_length = example
    seq_len = query_per_head.shape[0]
    inv_root = query_per_head.shape[-1] ** (-0.5)
    scores = (
        jnp.einsum("qhc,khc->hqk", query_per_head, key_heads, preferred_element_type=jnp.float32)
        * inv_root
    )
    query_pos = jnp.arange(seq_len, dtype=jnp.int32)[:, None]
    key_pos = jnp.arange(seq_len, dtype=jnp.int32)[None, :]
    allowed = (key_pos <= query_pos) & (key_pos < seq_length)
    scores = jnp.where(allowed[None], scores, masked_score)
    row_max = jnp.max(scores, axis=-1, keepdims=True)
    expon = jnp.exp(scores - row_max)
    attention = expon / jnp.sum(expon, axis=-1, keepdims=True)
    attention_low = attention.astype(jnp.bfloat16)
    grad_values = jnp.einsum(
        "hqk,qhc->khc", attention_low, grad_out, preferred_element_type=jnp.float32
    )
    grad_attention = jnp.einsum(
        "qhc,khc->hqk", grad_out, value_per_head, preferred_element_type=jnp.float32
    )
    inner_sum = jnp.sum(attention * grad_attention, axis=-1, keepdims=True)
    grad_scores = (attention * (grad_attention - inner_sum)).astype(jnp.bfloat16)
    grad_query = (
        jnp.einsum("hqk,khc->qhc", grad_scores, key_heads, preferred_element_type=jnp.float32)
        * inv_root
    )
    return (grad_query, grad_values)


def body(
    hidden,
    query_projection_matrix,
    key_projection_matrix,
    value_projection_matrix,
    adapter_down_maps,
    adapter_up_maps,
    cotangent,
    lengths,
    random_signs_down,
    random_signs_up,
):
    seq_count, seq_len, model_width = hidden.shape
    local_cols = query_projection_matrix.shape[1]
    heads_local = local_cols // HEAD_DIM
    token_matrix = hidden.reshape(seq_count * seq_len, model_width)

    def add_rows(weight_piece):
        return jnp.dot(token_matrix, weight_piece, preferred_element_type=jnp.float32)

    parts_dp = lax.axis_size(DP_AXES)
    local_rows = jnp.concatenate(
        [query_projection_matrix, key_projection_matrix, value_projection_matrix], axis=1
    )
    partner_rows = lax.ppermute(local_rows, "zl", [(0, 1), (1, 0)])
    low_first = lax.axis_index("zl") == 0
    pair_rows = jnp.stack(
        [
            jnp.where(low_first, local_rows, partner_rows),
            jnp.where(low_first, partner_rows, local_rows),
        ]
    )
    all_rows = lax.all_gather(pair_rows, ("x", "y"), axis=1, tiled=False).reshape(
        -1, local_rows.shape[1]
    )
    projected = add_rows(all_rows)
    plain_query = projected[:, :local_cols]
    base_key = projected[:, local_cols : 2 * local_cols]
    plain_value = projected[:, 2 * local_cols :]
    rotary_cosines, rotary_sines = rope_tables(seq_len, HEAD_DIM)
    inner_hidden = jnp.einsum(
        "no,wio->nwi", token_matrix, adapter_down_maps, preferred_element_type=jnp.float32
    ).astype(jnp.bfloat16)
    raised_features = jnp.einsum(
        "kdg,dgj->kdj", inner_hidden, adapter_up_maps, preferred_element_type=jnp.float32
    )
    head_layout = (seq_count, seq_len, heads_local, HEAD_DIM)
    query_per_head = apply_rotary(
        (plain_query + adapter_scale * raised_features[:, 0]).reshape(head_layout),
        rotary_cosines,
        rotary_sines,
    ).astype(jnp.bfloat16)
    key_heads = apply_rotary(base_key.reshape(head_layout), rotary_cosines, rotary_sines).astype(
        jnp.bfloat16
    )
    value_per_head = (
        (plain_value + adapter_scale * raised_features[:, 1])
        .astype(jnp.bfloat16)
        .reshape(head_layout)
    )
    valid = jnp.arange(seq_len, dtype=jnp.int32)[None, :] < lengths[:, None]
    masked_out = jnp.where(valid[:, :, None], cotangent, jnp.zeros_like(cotangent)).reshape(
        head_layout
    )
    grad_query, grad_values = lax.map(
        attention_grads, (query_per_head, key_heads, value_per_head, masked_out, lengths)
    )
    grad_query = (
        unrotate(grad_query, rotary_cosines, rotary_sines)
        .astype(jnp.bfloat16)
        .reshape(seq_count, seq_len, local_cols)
    )
    grad_values = grad_values.astype(jnp.bfloat16).reshape(seq_count, seq_len, local_cols)
    per_head_gradient = jnp.stack([grad_query, grad_values], axis=2)
    branch_portion = jnp.einsum(
        "liov,ohv->lioh", per_head_gradient, adapter_up_maps, preferred_element_type=jnp.float32
    )
    adapter_branch = jnp.sum(
        lax.all_gather(branch_portion, TP_AXES, axis=0, tiled=False), axis=0
    ).astype(jnp.bfloat16)
    middle_seq = inner_hidden.reshape(seq_count, seq_len, 2, ADAPTER_RANK)
    up_map_gradient = adapter_scale * jnp.einsum(
        "esar,esac->earc", middle_seq, per_head_gradient, preferred_element_type=jnp.float32
    )
    parts_tensor = lax.axis_size(TP_AXES)
    row_block = model_width // (parts_dp * parts_tensor)
    hidden_blocks = hidden.reshape(seq_count, seq_len, parts_dp, parts_tensor, row_block)
    local_column_range = lax.dynamic_index_in_dim(
        hidden_blocks, lax.axis_index(TP_AXES), axis=3, keepdims=False
    )
    down_map_local = adapter_scale * jnp.einsum(
        "ykzu,ykhc->yhzuc", adapter_branch, local_column_range, preferred_element_type=jnp.float32
    )
    down_map_local = down_map_local.reshape(seq_count, parts_dp, 1, 2 * ADAPTER_RANK * row_block)
    slice_len = HEAD_DIM // parts_dp
    up_blocks = up_map_gradient.reshape(
        seq_count, 2, ADAPTER_RANK, heads_local, parts_dp, slice_len
    )
    up_blocks = up_blocks.transpose(0, 4, 1, 2, 3, 5).reshape(
        seq_count, parts_dp, 1, 2 * ADAPTER_RANK * heads_local * slice_len
    )
    packed = jnp.concatenate([down_map_local, up_blocks], axis=3).astype(jnp.bfloat16)
    routed = lax.all_to_all(packed, DP_AXES, split_axis=1, concat_axis=0, tiled=True)
    gathered = routed.reshape(routed.shape[0], routed.shape[3])
    down_count = down_map_local.shape[3]
    down_table = random_signs_down.reshape(down_count, random_signs_down.shape[-1])
    up_table = random_signs_up.reshape(gathered.shape[1] - down_count, random_signs_up.shape[-1])
    partial = (
        jnp.dot(gathered[:, :down_count], down_table, preferred_element_type=jnp.float32)
        + jnp.dot(gathered[:, down_count:], up_table, preferred_element_type=jnp.float32)
    ).astype(jnp.bfloat16)
    own_count = partial.shape[0] // parts_dp
    feat_block = partial.shape[1] // parts_tensor
    blocks = partial.reshape(parts_dp, own_count, parts_tensor, feat_block).transpose(0, 2, 1, 3)
    to_owner = lax.all_to_all(
        blocks.reshape(parts_dp * parts_tensor, own_count, feat_block),
        DP_AXES + TP_AXES,
        0,
        0,
        tiled=True,
    )
    features_local = jnp.sum(to_owner.astype(jnp.float32), axis=0)
    squares = lax.psum(jnp.sum(features_local * features_local, axis=1), TP_AXES)
    return features_local * lax.rsqrt(squares / FEAT + norm_eps)[:, None]


def solution(mesh):
    fine_mesh = Mesh(mesh.devices.reshape(2, 4, 4, 2, 2), ("zl", "x", "y", "zh", "core"))
    return jax.shard_map(
        body,
        mesh=fine_mesh,
        in_specs=(
            P(DP_AXES, None, None),
            P(DP_AXES, TP_AXES),
            P(DP_AXES, TP_AXES),
            P(DP_AXES, TP_AXES),
            P(),
            P(None, None, TP_AXES),
            P(DP_AXES, None, TP_AXES),
            P(DP_AXES),
            P(None, None, DP_AXES + TP_AXES, None),
            P(None, None, TP_AXES, DP_AXES, None),
        ),
        out_specs=P(DP_AXES, TP_AXES),
        check_vma=False,
    )
```

profile of v0, /device:TPU:0, one launch (start us, length us, event | category | flops | bytes accessed | tf_op | source)
XLA Modules:
  0.0 321.8 jit_solution(1688211024387175101)
XLA Ops:
  11.6 13.9 %collective-permute-done = bf16[160,1920]{1,0:T(8,128)(2,1)S(1)} collective-permute-done((bf16[160,1920]{1,0:T(8,128)(2,1)S(1)}, bf16[160,1920]{1,0:T(8,128)(2,1)S(1)}, u32[]{:S(2)}, u32[]{:S(2)}) %collective-permute-start) | collective-permute-done | bytes 614432 | tf_op jit(solution)/shard_map/ppermute | solution.py:94
  27.4 14.0 %copy.61 = bf16[2,512,5120]{1,2,0:T(8,128)(2,1)} copy(bf16[2,512,5120]{2,1,0:T(8,128)(2,1)} %param.12) | data formatting | bytes 20971520 | tf_op args[0]
  43.3 6.8 %convolution_convert_fusion = bf16[1024,2,8]{0,2,1:T(8,128)(2,1)S(1)} fusion(bf16[1024,5120,1]{1,0,2:T(8,128)(2,1)} %bitcast.140, bf16[2,8,5120]{2,1,0:T(8,128)(2,1)S(1)} %copy-done), kind=kOutput, calls=%fused_computation.79 | convolution fusion | flops 167788544 | bytes 10682368 | tf_op jit(solution)/shard_map/no,wio->nwi/dot_general | solution.py:110
  50.8 3.2 convolution_bitcast_fusion.1
  53.9 101.0 %all-gather.4.cloned.1.call-done = bf16[2,2560,1920]{2,1,0:T(8,128)(2,1)} async-done(((bf16[2,160,1920]{2,1,0:T(8,128)(2,1)}), bf16[2,2560,1920]{2,1,0:T(8,128)(2,1)}) %all-gather.4.cloned.1.call-update) | async-done | bytes 19660816 | tf_op jit(solution)/shard_map/all_gather | solution.py:102
  154.9 28.5 %convolution_bitcast_fusion = f32[1024,1920]{0,1:T(8,128)} fusion(bf16[5120,1920]{1,0:T(8,128)(2,1)} %bitcast.153, bf16[1024,5120]{1,0:T(8,128)(2,1)} %bitcast.141), kind=kOutput, calls=%fused_computation.44 | convolution fusion | flops 20132659200 | bytes 38010880 | tf_op jit(solution)/shard_map/dot_general | solution.py:88
  183.4 8.6 %fusion.42 = (bf16[1024,640]{0,1:T(8,128)(2,1)}, f32[1024,640]{0,1:T(8,128)}, f32[1024,640]{0,1:T(8,128)}) fusion(f32[1024,2,640]{0,2,1:T(8,128)} %convolution_bitcast_fusion.1, f32[1024,1920]{0,1:T(8,128)} %convolution_bitcast_fusion), kind=kLoop, calls=%fused_computation.48 | loop fusion | flops 3276800 | bytes 19660800 | tf_op jit(solution)/shard_map/convert_element_type | solution.py:127
  192.1 3.7 %reshape.155 = f32[2,512,5,128]{1,0,3,2:T(2,128)S(1)} reshape(f32[1024,640]{0,1:T(8,128)} %get-tuple-element.96) | data formatting | bytes 5242880 | tf_op jit(solution)/shard_map/reshape | solution.py:122
  197.7 4.8 %reshape.156 = f32[2,512,5,128]{1,0,3,2:T(2,128)} reshape(f32[1024,640]{0,1:T(8,128)} %get-tuple-element.95) | data formatting | bytes 5242880 | tf_op jit(solution)/shard_map/reshape | solution.py:118
  202.5 3.8 %copy.66 = f32[2,512,5,128]{1,3,2,0:T(8,128)} copy(f32[2,512,5,128]{1,0,3,2:T(2,128)} %reshape.156) | data formatting | bytes 5242880 | tf_op jit(solution)/shard_map/reshape | solution.py:118
  206.3 4.4 %reshape.158 = bf16[2,512,5,128]{1,0,3,2:T(2,128)(2,1)} reshape(bf16[1024,640]{0,1:T(8,128)(2,1)} %get-tuple-element.94) | data formatting | bytes 2621440 | tf_op jit(solution)/shard_map/reshape | solution.py:128
  210.7 4.3 %copy.73 = bf16[2,512,5,128]{3,1,2,0:T(8,128)(2,1)} copy(bf16[2,512,5,128]{1,0,3,2:T(2,128)(2,1)} %reshape.158) | data formatting | bytes 2621440 | tf_op jit(solution)/shard_map/while | solution.py:134
  215.0 3.4 %slice_negate_fusion.1 = (f32[2,512,5,64]{1,3,2,0:T(8,128)S(1)}, f32[2,512,5,64]{1,3,2,0:T(8,128)S(1)}, f32[2,512,5,64]{1,3,2,0:T(8,128)S(1)}, f32[2,512,5,64]{1,3,2,0:T(8,128)S(1)}) fusion(f32[2,512,5,128]{1,3,2,0:T(8,128)} %copy.66, f32[2,512,5,128]{1,3,2,0:T(8,128)} %copy.62), kind=kLoop, calls=%fused_computation.68 | loop fusion | flops 655360 | bytes 10485760 | tf_op jit(solution)/shard_map/neg | solution.py:28
  218.3 2.7 fusion.48
  221.0 22.2 %while.12 = (s32[]{:T(128)}, f32[2,512,5,128]{1,3,2,0:T(8,128)}, bf16[2,512,5,128]{1,3,2,0:T(8,128)(2,1)}, bf16[2,512,5,128]{1,3,2,0:T(8,128)(2,1)}, s32[2]{0:T(...) while((s32[]{:T(128)}, f32[2,512,5,128]{1,3,2,0:T(8,128)}, ...), condition=%wide.region_4.5_spmd, body=%wide.region_0.4_spmd.sunk | while | flops 1362688512 | bytes 75326712 | solution.py:134
  224.6 2.5 fusion.107
  253.2 7.5 %all-gather.1 = f32[8,512,2,8]{1,3,0,2:T(8,128)S(1)} all-gather(f32[2,512,2,8]{1,3,0,2:T(8,128)S(1)} %convolution_bitcast_fusion.2), channel_id=3, replica_groups=mesh['zl'=2,'x'=4,'y'=4,'zh'=2,'core'=2] {'zh','core'}, dimensions={0}, use_global_device_ids=true | all-gather | bytes 327680 | tf_op jit(solution)/shard_map/all_gather | solution.py:148
  260.7 3.3 %fusion.61 = bf16[2,32,2,8,40]{4,3,2,1,0:T(8,128)(2,1)S(1)} fusion(bf16[2,512,32,4,40]{1,4,3,2,0:T(8,128)(2,1)} %bitcast.142, s32[]{:T(128)S(6)} %select_n.24, bf16[2,512,2,8]{1,3,0,2:T(8,128)(2,1)S(1)} %reduce_sum.45), kind=kOutput, calls=%fused_computation.75 | convolution fusion | flops 42024960 | bytes 2736132 | tf_op jit(solution)/shard_map/ykzu,ykhc->yhzuc/dot_general | solution.py:160
  266.5 6.4 %all-to-all-start = ((bf16[2,32,1,960]{3,0,2,1:T(2,128)(2,1)}), bf16[2,32,1,960]{3,0,2,1:T(2,128)(2,1)S(1)}, u32[]{:S(2)}, u32[]{:S(2)}) async-start(bf16[2,32,1,960]{3,0,2,1:T(2,128)(2,1)} %pad_maximum_fusion.4), calls=%async_computation | async-start | bytes 262144 | tf_op jit(solution)/shard_map/all_to_all | solution.py:172
  272.9 3.5 %reshape.163 = bf16[320,4096]{1,0:T(8,128)(2,1)S(1)} reshape(bf16[2,8,5,4,4096]{4,3,2,1,0:T(4,128)(2,1)} %param.21) | data formatting | bytes 5242880 | tf_op jit(solution)/shard_map/reshape | solution.py:176
  276.5 5.0 %all-to-all-done = bf16[2,32,1,960]{3,0,2,1:T(2,128)(2,1)S(1)} async-done(((bf16[2,32,1,960]{3,0,2,1:T(2,128)(2,1)}), bf16[2,32,1,960]{3,0,2,1:T(2,128)(2,1)S(1)}, u32[]{:S(2)}, u32[]{:S(2)}) %all-to-all-start) | async-done | bytes 122912 | tf_op jit(solution)/shard_map/all_to_all | solution.py:172
  281.6 3.5 %fusion.72 = f32[64,4096]{1,0:T(8,128)S(1)} fusion(bf16[640,4096]{1,0:T(8,128)(2,1)} %bitcast.143, bf16[64,960]{1,0:T(8,128)(2,1)S(1)} %reshape.161), kind=kOutput, calls=%fused_computation.89 | convolution fusion | flops 335544320 | bytes 6373376 | tf_op jit(solution)/shard_map/dot_general | solution.py:178
  286.7 18.9 %all_to_all.20 = bf16[128,2,1024]{2,1,0:T(2,128)(2,1)S(1)} all-to-all(bf16[128,2,1024]{2,1,0:T(2,128)(2,1)S(1)} %bitcast.146), channel_id=1, replica_groups=mesh['zl'=2,'x'=4,'y'=4,'zh'=2,'core'=2] {'zl','x','y','zh','core'}, dimensions={0} | all-to-all | bytes 1048576 | tf_op jit(solution)/shard_map/all_to_all | solution.py:184
  306.2 8.1 %psum.7 = f32[2]{0:T(128)S(1)} all-reduce(f32[2]{0:T(128)S(1)} %multiply_reduce_fusion.1), channel_id=1, replica_groups=mesh['zl'=2,'x'=4,'y'=4,'zh'=2,'core'=2] {'zh','core'}, use_global_device_ids=true, to_apply=%region_8.9 | all-reduce | flops 2 | bytes 16 | tf_op jit(solution)/shard_map/psum | solution.py:192
  (98 shorter events, 46.2 us)
Async XLA Ops:
  6.5 36.8 %copy-start = (bf16[2,8,5120]{2,1,0:T(8,128)(2,1)S(1)}, bf16[2,8,5120]{2,1,0:T(8,128)(2,1)}, u32[]{:S(2)}) copy-start(bf16[2,8,5120]{2,1,0:T(8,128)(2,1)} %param.16) | copy-start | bytes 491524
  6.5 148.4 %all-gather.4.cloned.1.call-start = ((), (), s32[]{:S(2)}) async-start(), calls=%async_computation.2 | async-start | bytes 20889600 | tf_op jit(solution)/shard_map/all_gather | solution.py:102
  9.4 16.0 %collective-permute-start = (bf16[160,1920]{1,0:T(8,128)(2,1)S(1)}, bf16[160,1920]{1,0:T(8,128)(2,1)S(1)}, u32[]{:S(2)}, u32[]{:S(2)}) collective-permute-start(bf16[160,1920]{1,0:T(8,128)(2,1)S(1)} %constant_dynamic-update-slice_fusion), channel_id=1, source_target_pairs={{0,64},{64,0},{1,65},{65,1},{2,66},{66,2},{3,67},{67,3},{4,68},{68... | collective-permute-start | bytes 1843208 | tf_op jit(solution)/shard_map/ppermute | solution.py:94
  11.6 15.2 %copy-start.4 = (bf16[2,512,640]{2,1,0:T(8,128)(2,1)S(1)}, bf16[2,512,640]{2,1,0:T(8,128)(2,1)}, u32[]{:S(2)}) copy-start(bf16[2,512,640]{2,1,0:T(8,128)(2,1)} %param.18) | copy-start | bytes 3932164
  27.4 14.6 %copy-start.16 = (s32[2]{0:T(128)S(1)}, s32[2]{0:T(128)}, u32[]{:S(2)}) copy-start(s32[2]{0:T(128)} %param.19) | copy-start | bytes 28
  43.3 7.4 %copy-start.14 = (bf16[2,8,640]{2,1,0:T(8,128)(2,1)S(1)}, bf16[2,8,640]{2,1,0:T(8,128)(2,1)}, u32[]{:S(2)}) copy-start(bf16[2,8,640]{2,1,0:T(8,128)(2,1)} %param.17) | copy-start | bytes 61444
  215.0 3.4 %copy-start.2 = (f32[2,512,5,128]{1,0,3,2:T(2,128)S(1)}, f32[2,512,5,128]{1,0,3,2:T(2,128)}, u32[]{:S(2)}) copy-start(f32[2,512,5,128]{1,0,3,2:T(2,128)} %reshape.156) | copy-start | bytes 7864324
  224.6 2.6 copy-start.5
  224.6 2.6 copy-start.11
  227.2 1.3 copy-start.8
  228.2 1.2 copy-start.6
  228.5 1.5 copy-start.3
  235.7 2.6 copy-start.5
  235.7 2.6 copy-start.11
  238.3 1.3 copy-start.8
  239.3 1.2 copy-start.6
  239.6 1.5 copy-start.3
  248.1 1.5 copy-start.7
  248.1 2.9 copy-start.15
  249.6 1.5 copy-start.9
  253.2 11.2 %copy-start.10 = (bf16[2,512,1,640]{3,1,0,2:T(8,128)(2,1)S(1)}, bf16[2,512,1,640]{3,1,0,2:T(8,128)(2,1)}, u32[]{:S(2)}) copy-start(bf16[2,512,1,640]{3,1,0,2:T(8,128)(2,1)} %copy.75) | copy-start | bytes 3932164
  253.2 11.2 %copy-start.13 = (bf16[1024,2,8]{0,2,1:T(8,128)(2,1)S(1)}, bf16[1024,2,8]{0,2,1:T(8,128)(2,1)}, u32[]{:S(2)}) copy-start(bf16[1024,2,8]{0,2,1:T(8,128)(2,1)} %copy-done.12) | copy-start | bytes 98308
  266.5 15.0 %all-to-all-start = ((bf16[2,32,1,960]{3,0,2,1:T(2,128)(2,1)}), bf16[2,32,1,960]{3,0,2,1:T(2,128)(2,1)S(1)}, u32[]{:S(2)}, u32[]{:S(2)}) async-start(bf16[2,32,1,960]{3,0,2,1:T(2,128)(2,1)} %pad_maximum_fusion.4), calls=%async_computation | async-start | bytes 262144 | tf_op jit(solution)/shard_map/all_to_all | solution.py:172
  285.1 29.9 %copy-start.1 = (bf16[2,8,5120]{2,1,0:T(8,128)(2,1)S(1)}, bf16[2,8,5120]{2,1,0:T(8,128)(2,1)}, u32[]{:S(2)}) copy-start(bf16[2,8,5120]{2,1,0:T(8,128)(2,1)} %param.16) | copy-start | bytes 491524
  (1 other events, 0.6 us)
Sparse Core Ops, SparseCore 0:
  26.9 127.9 all-gather.3
where the time goes:
time: 323 us; the launch traced here: 322 us
  waiting for transfers between devices  120 us (37%)
  matrix products  61 us (19%)
  local copies, waits for them, and re-layouts  52.8 us (16%)
  blocking collectives  34.5 us (11%)
  other arithmetic  31.3 us (10%)
  between operations  13.7 us (4%)
  starting transfers between devices  8.52 us (3%)
    all_gather x1, waiting for transfers between devices, body(): lax.all_gather(pair_rows, ('x', 'y'), axis=1, tiled=False)  101 us
    dot_general x1, matrix products, add_rows(): jnp.dot(token_matrix, weight_piece, preferred_element_type=jnp.float32)  28.5 us
    all_to_all x1, blocking collectives, body(): lax.all_to_all(blocks.reshape(parts_dp * parts_tensor, own_count, feat_bl...  18.9 us
    unnamed x28, local copies, waits for them, and re-layouts  17.3 us
    ppermute x1, waiting for transfers between devices, body(): partner_rows = lax.ppermute(local_rows, 'zl', [(0, 1), (1, 0)])  13.9 us
    convert_element_type x1, other arithmetic, body(): value_per_head = (plain_value + adapter_scale * raised_features[:, 1]).as...  8.62 us
    reshape x2, local copies, waits for them, and re-layouts, body(): (plain_query + adapter_scale * raised_features[:, 0]).reshape(head_layout)  8.61 us
    psum x1, blocking collectives, body(): lax.psum(jnp.sum(features_local * features_local, axis=1), TP_AXES)  8.1 us
  transfers between devices with their start and end apart: 3, of which 3 were waited for; matrix products, arithmetic and copies ran while one was open for 9% of the time, Pallas kernels for 0%

commit v1 on v0

--- a/solution.py
+++ b/solution.py
@@ -169,7 +169,10 @@
         seq_count, parts_dp, 1, 2 * ADAPTER_RANK * heads_local * slice_len
     )
     packed = jnp.concatenate([down_map_local, up_blocks], axis=3).astype(jnp.bfloat16)
-    routed = lax.all_to_all(packed, DP_AXES, split_axis=1, concat_axis=0, tiled=True)
+    peers = lax.axis_size(DP_AXES)
+    pieces = jnp.stack(jnp.split(packed, peers, axis=1), axis=0)
+    pieces = lax.all_to_all(pieces, DP_AXES, split_axis=0, concat_axis=0)
+    routed = jnp.concatenate(pieces, axis=0)
     gathered = routed.reshape(routed.shape[0], routed.shape[3])
     down_count = down_map_local.shape[3]
     down_table = random_signs_down.reshape(down_count, random_signs_down.shape[-1])

time: 323 us -> 342 us (1.059)
  other arithmetic: 31.3 us -> 49.6 us
    unnamed x0 -> x31, other arithmetic: none -> 18.5 us
where the time goes in v1:
time: 342 us; the launch traced here: 340 us
  waiting for transfers between devices  120 us (35%)
  matrix products  61 us (18%)
  local copies, waits for them, and re-layouts  52.8 us (15%)
  other arithmetic  49.6 us (15%)
  blocking collectives  34.5 us (10%)
  between operations  13.7 us (4%)
  starting transfers between devices  8.52 us (2%)
    all_gather x1, waiting for transfers between devices, body(): lax.all_gather(pair_rows, ('x', 'y'), axis=1, tiled=False)  101 us
    dot_general x1, matrix products, add_rows(): jnp.dot(token_matrix, weight_piece, preferred_element_type=jnp.float32)  28.5 us
    all_to_all x1, blocking collectives, body(): lax.all_to_all(blocks.reshape(parts_dp * parts_tensor, own_count, feat_bl...  18.9 us
    unnamed x31, other arithmetic  18.5 us
    unnamed x28, local copies, waits for them, and re-layouts  17.3 us
    ppermute x1, waiting for transfers between devices, body(): partner_rows = lax.ppermute(local_rows, 'zl', [(0, 1), (1, 0)])  13.9 us
    convert_element_type x1, other arithmetic, body(): value_per_head = (plain_value + adapter_scale * raised_features[:, 1]).as...  8.62 us
    reshape x2, local copies, waits for them, and re-layouts, body(): (plain_query + adapter_scale * raised_features[:, 0]).reshape(head_layout)  8.61 us
  transfers between devices with their start and end apart: 3, of which 3 were waited for; matrix products, arithmetic and copies ran while one was open for 9% of the time, Pallas kernels for 0%

profile of v1, /device:TPU:0, one launch (start us, length us, event | category | flops | bytes accessed | tf_op | source)
XLA Modules:
  0.0 340.2 jit_solution(14164976010924299691)
XLA Ops:
  11.6 13.9 %collective-permute-done = bf16[160,1920]{1,0:T(8,128)(2,1)S(1)} collective-permute-done((bf16[160,1920]{1,0:T(8,128)(2,1)S(1)}, bf16[160,1920]{1,0:T(8,128)(2,1)S(1)}, u32[]{:S(2)}, u32[]{:S(2)}) %collective-permute-start) | collective-permute-done | bytes 614432 | tf_op jit(solution)/shard_map/ppermute | solution.py:94
  27.4 14.0 %copy.92 = bf16[2,512,5120]{1,2,0:T(8,128)(2,1)} copy(bf16[2,512,5120]{2,1,0:T(8,128)(2,1)} %param.12) | data formatting | bytes 20971520 | tf_op args[0]
  43.3 6.8 %convolution_convert_fusion = bf16[1024,2,8]{0,2,1:T(8,128)(2,1)S(1)} fusion(bf16[1024,5120,1]{1,0,2:T(8,128)(2,1)} %bitcast.265, bf16[2,8,5120]{2,1,0:T(8,128)(2,1)S(1)} %copy-done), kind=kOutput, calls=%fused_computation.79 | convolution fusion | flops 167788544 | bytes 10682368 | tf_op jit(solution)/shard_map/no,wio->nwi/dot_general | solution.py:110
  50.8 3.2 convolution_bitcast_fusion.1
  53.9 101.0 %all-gather.4.cloned.1.call-done = bf16[2,2560,1920]{2,1,0:T(8,128)(2,1)} async-done(((bf16[2,160,1920]{2,1,0:T(8,128)(2,1)}), bf16[2,2560,1920]{2,1,0:T(8,128)(2,1)}) %all-gather.4.cloned.1.call-update) | async-done | bytes 19660816 | tf_op jit(solution)/shard_map/all_gather | solution.py:102
  154.9 28.5 %convolution_bitcast_fusion = f32[1024,1920]{0,1:T(8,128)} fusion(bf16[5120,1920]{1,0:T(8,128)(2,1)} %bitcast.277, bf16[1024,5120]{1,0:T(8,128)(2,1)} %bitcast.266), kind=kOutput, calls=%fused_computation.44 | convolution fusion | flops 20132659200 | bytes 38010880 | tf_op jit(solution)/shard_map/dot_general | solution.py:88
  183.4 8.6 %fusion.42 = (bf16[1024,640]{0,1:T(8,128)(2,1)}, f32[1024,640]{0,1:T(8,128)}, f32[1024,640]{0,1:T(8,128)}) fusion(f32[1024,2,640]{0,2,1:T(8,128)} %convolution_bitcast_fusion.1, f32[1024,1920]{0,1:T(8,128)} %convolution_bitcast_fusion), kind=kLoop, calls=%fused_computation.48 | loop fusion | flops 3276800 | bytes 19660800 | tf_op jit(solution)/shard_map/convert_element_type | solution.py:127
  192.1 3.7 %reshape.151 = f32[2,512,5,128]{1,0,3,2:T(2,128)S(1)} reshape(f32[1024,640]{0,1:T(8,128)} %get-tuple-element.96) | data formatting | bytes 5242880 | tf_op jit(solution)/shard_map/reshape | solution.py:122
  197.7 4.8 %reshape.152 = f32[2,512,5,128]{1,0,3,2:T(2,128)} reshape(f32[1024,640]{0,1:T(8,128)} %get-tuple-element.95) | data formatting | bytes 5242880 | tf_op jit(solution)/shard_map/reshape | solution.py:118
  202.5 3.8 %copy.97 = f32[2,512,5,128]{1,3,2,0:T(8,128)} copy(f32[2,512,5,128]{1,0,3,2:T(2,128)} %reshape.152) | data formatting | bytes 5242880 | tf_op jit(solution)/shard_map/reshape | solution.py:118
  206.3 4.4 %reshape.154 = bf16[2,512,5,128]{1,0,3,2:T(2,128)(2,1)} reshape(bf16[1024,640]{0,1:T(8,128)(2,1)} %get-tuple-element.94) | data formatting | bytes 2621440 | tf_op jit(solution)/shard_map/reshape | solution.py:128
  210.7 4.3 %copy.104 = bf16[2,512,5,128]{3,1,2,0:T(8,128)(2,1)} copy(bf16[2,512,5,128]{1,0,3,2:T(2,128)(2,1)} %reshape.154) | data formatting | bytes 2621440 | tf_op jit(solution)/shard_map/while | solution.py:134
  215.0 3.4 slice_negate_fusion.1
  218.3 2.7 fusion.48
  221.0 22.2 %while.12 = (s32[]{:T(128)}, f32[2,512,5,128]{1,3,2,0:T(8,128)}, bf16[2,512,5,128]{1,3,2,0:T(8,128)(2,1)}, bf16[2,512,5,128]{1,3,2,0:T(8,128)(2,1)}, s32[2]{0:T(...) while((s32[]{:T(128)}, f32[2,512,5,128]{1,3,2,0:T(8,128)}, ...), condition=%wide.region_4.5_spmd, body=%wide.region_0.4_spmd.sunk | while | flops 1362688512 | bytes 75326712 | solution.py:134
  224.6 2.5 fusion.108
  253.2 7.5 %all-gather.1 = f32[8,512,2,8]{1,3,0,2:T(8,128)S(1)} all-gather(f32[2,512,2,8]{1,3,0,2:T(8,128)S(1)} %convolution_bitcast_fusion.2), channel_id=3, replica_groups=mesh['zl'=2,'x'=4,'y'=4,'zh'=2,'core'=2] {'zh','core'}, dimensions={0}, use_global_device_ids=true | all-gather | bytes 327680 | tf_op jit(solution)/shard_map/all_gather | solution.py:148
  260.7 3.3 fusion.61
  284.9 6.4 %all-to-all-start = ((bf16[32,2,1,1,960]{4,1,3,2,0:T(2,128)(2,1)}), bf16[32,2,1,1,960]{4,1,3,2,0:T(2,128)(2,1)S(1)}, u32[]{:S(2)}, u32[]{:S(2)}) async-start(bf16[32,2,1,1,960]{4,1,3,2,0:T(2,128)(2,1)} %constant_dynamic-update-slice_fusion.3), calls=%async_computation | async-start | bytes 262144 | tf_op jit(solution)/shard_map/all_to_all | solution.py:174
  291.3 3.5 %reshape.158 = bf16[320,4096]{1,0:T(8,128)(2,1)S(1)} reshape(bf16[2,8,5,4,4096]{4,3,2,1,0:T(4,128)(2,1)} %param.21) | data formatting | bytes 5242880 | tf_op jit(solution)/shard_map/reshape | solution.py:179
  294.8 5.0 %all-to-all-done = bf16[32,2,1,1,960]{4,1,3,2,0:T(2,128)(2,1)S(1)} async-done(((bf16[32,2,1,1,960]{4,1,3,2,0:T(2,128)(2,1)}), bf16[32,2,1,1,960]{4,1,3,2,0:T(2,128)(2,1)S(1)}, u32[]{:S(2)}, u32[]{:S(2)}) %all-to-all-start) | async-done | bytes 122912 | tf_op jit(solution)/shard_map/all_to_all | solution.py:174
  299.9 3.5 %fusion.72 = f32[64,4096]{1,0:T(8,128)S(1)} fusion(bf16[640,4096]{1,0:T(8,128)(2,1)} %bitcast.268, bf16[64,960]{1,0:T(8,128)(2,1)S(1)} %reshape_reshape.3), kind=kOutput, calls=%fused_computation.88 | convolution fusion | flops 335544320 | bytes 6373376 | tf_op jit(solution)/shard_map/dot_general | solution.py:181
  305.1 18.9 %all_to_all.10 = bf16[128,2,1024]{2,1,0:T(2,128)(2,1)S(1)} all-to-all(bf16[128,2,1024]{2,1,0:T(2,128)(2,1)S(1)} %bitcast.271), channel_id=1, replica_groups=mesh['zl'=2,'x'=4,'y'=4,'zh'=2,'core'=2] {'zl','x','y','zh','core'}, dimensions={0} | all-to-all | bytes 1048576 | tf_op jit(solution)/shard_map/all_to_all | solution.py:187
  324.6 8.1 %psum.7 = f32[2]{0:T(128)S(1)} all-reduce(f32[2]{0:T(128)S(1)} %multiply_reduce_fusion.1), channel_id=1, replica_groups=mesh['zl'=2,'x'=4,'y'=4,'zh'=2,'core'=2] {'zh','core'}, use_global_device_ids=true, to_apply=%region_8.9 | all-reduce | flops 2 | bytes 16 | tf_op jit(solution)/shard_map/psum | solution.py:195
  (129 shorter events, 64.6 us)
Async XLA Ops:
  6.5 36.8 %copy-start = (bf16[2,8,5120]{2,1,0:T(8,128)(2,1)S(1)}, bf16[2,8,5120]{2,1,0:T(8,128)(2,1)}, u32[]{:S(2)}) copy-start(bf16[2,8,5120]{2,1,0:T(8,128)(2,1)} %param.16) | copy-start | bytes 491524
  6.5 148.4 %all-gather.4.cloned.1.call-start = ((), (), s32[]{:S(2)}) async-start(), calls=%async_computation.2 | async-start | bytes 20889600 | tf_op jit(solution)/shard_map/all_gather | solution.py:102
  9.4 16.0 %collective-permute-start = (bf16[160,1920]{1,0:T(8,128)(2,1)S(1)}, bf16[160,1920]{1,0:T(8,128)(2,1)S(1)}, u32[]{:S(2)}, u32[]{:S(2)}) collective-permute-start(bf16[160,1920]{1,0:T(8,128)(2,1)S(1)} %constant_dynamic-update-slice_fusion), channel_id=1, source_target_pairs={{0,64},{64,0},{1,65},{65,1},{2,66},{66,2},{3,67},{67,3},{4,68},{68... | collective-permute-start | bytes 1843208 | tf_op jit(solution)/shard_map/ppermute | solution.py:94
  11.6 15.2 %copy-start.4 = (bf16[2,512,640]{2,1,0:T(8,128)(2,1)S(1)}, bf16[2,512,640]{2,1,0:T(8,128)(2,1)}, u32[]{:S(2)}) copy-start(bf16[2,512,640]{2,1,0:T(8,128)(2,1)} %param.18) | copy-start | bytes 3932164
  27.4 14.6 %copy-start.16 = (s32[2]{0:T(128)S(1)}, s32[2]{0:T(128)}, u32[]{:S(2)}) copy-start(s32[2]{0:T(128)} %param.19) | copy-start | bytes 28
  43.3 7.4 %copy-start.14 = (bf16[2,8,640]{2,1,0:T(8,128)(2,1)S(1)}, bf16[2,8,640]{2,1,0:T(8,128)(2,1)}, u32[]{:S(2)}) copy-start(bf16[2,8,640]{2,1,0:T(8,128)(2,1)} %param.17) | copy-start | bytes 61444
  215.0 3.4 copy-start.2
  224.6 2.6 copy-start.5
  224.6 2.6 copy-start.11
  227.2 1.3 copy-start.8
  228.2 1.2 copy-start.6
  228.5 1.5 copy-start.3
  235.7 2.6 copy-start.5
  235.7 2.6 copy-start.11
  238.3 1.3 copy-start.8
  239.3 1.2 copy-start.6
  239.6 1.5 copy-start.3
  248.1 1.5 copy-start.7
  248.1 2.9 copy-start.15
  249.6 1.5 copy-start.9
  253.2 11.2 %copy-start.10 = (bf16[2,512,1,640]{3,1,0,2:T(8,128)(2,1)S(1)}, bf16[2,512,1,640]{3,1,0,2:T(8,128)(2,1)}, u32[]{:S(2)}) copy-start(bf16[2,512,1,640]{3,1,0,2:T(8,128)(2,1)} %copy.106) | copy-start | bytes 3932164
  253.2 11.2 %copy-start.13 = (bf16[1024,2,8]{0,2,1:T(8,128)(2,1)S(1)}, bf16[1024,2,8]{0,2,1:T(8,128)(2,1)}, u32[]{:S(2)}) copy-start(bf16[1024,2,8]{0,2,1:T(8,128)(2,1)} %copy-done.12) | copy-start | bytes 98308
  284.9 15.0 %all-to-all-start = ((bf16[32,2,1,1,960]{4,1,3,2,0:T(2,128)(2,1)}), bf16[32,2,1,1,960]{4,1,3,2,0:T(2,128)(2,1)S(1)}, u32[]{:S(2)}, u32[]{:S(2)}) async-start(bf16[32,2,1,1,960]{4,1,3,2,0:T(2,128)(2,1)} %constant_dynamic-update-slice_fusion.3), calls=%async_computation | async-start | bytes 262144 | tf_op jit(solution)/shard_map/all_to_all | solution.py:174
  303.5 29.9 %copy-start.1 = (bf16[2,8,5120]{2,1,0:T(8,128)(2,1)S(1)}, bf16[2,8,5120]{2,1,0:T(8,128)(2,1)}, u32[]{:S(2)}) copy-start(bf16[2,8,5120]{2,1,0:T(8,128)(2,1)} %param.16) | copy-start | bytes 491524
  (1 other events, 0.6 us)
Sparse Core Ops, SparseCore 0:
  26.9 127.9 all-gather.3
